TPU v7x, 32 devices: a whole 2x2x4 slice. The times are simulated.
32 devices in a mesh: cam: 2 (over core), tile: 16 (over z, y, x).
Axes of the slice: x: 2, y: 2, z: 4, core: 2. Of those that a mesh axis runs over, the one named last changes fastest.
Arguments:
- queries: bfloat16 [4096, 256], P('tile'), as said below
- keys: bfloat16 [2048, 256], P(('cam', 'tile')), as said below
- values: bfloat16 [2048, 256], P(('cam', 'tile')), may hold values from -6 to 6
- grad_out: bfloat16 [4096, 256], P('tile'), may hold values from -6 to 6
- visible: int32 [32, 64], P('tile', 'cam'), may hold values from 0 to 1, as said below
- counts: int32 [64], P('cam'), may hold values from 2 to 32
Outputs:
- grad_queries: bfloat16 [4096, 256], P('tile')
- grad_keys: bfloat16 [2048, 256], P(('cam', 'tile'))
- grad_values: bfloat16 [2048, 256], P(('cam', 'tile'))
Inputs may be any that keep to these rules, and one draw needn't show every extreme that they name: Every tile has at least one visible block. `queries`: projected query features. `keys`: projected key features.
All inputs are finite; a program needn't handle non-finite values.
Results may differ from a plain program's by a relative error of at most 0.0052.
Values may be sent and summed in bfloat16 or wider, within the bound.
No kernel may reach another device: no remote copies, remote signals or barrier semaphores. Data moves between devices by JAX's collectives and lax.ppermute only.
A program may use at most 128 MiB of HBM per device.

v0:
```python
import math
import jax
import jax.numpy as jnp
from jax import lax
from jax.sharding import PartitionSpec as P

H = 8


def merged(array, axis, combine):
    everything = jax.tree.map(lambda part: lax.all_gather(part, axis), array)
    initial = jax.tree.map(lambda part: part[0], everything)

    def step(k, so_far):
        return combine(so_far, jax.tree.map(lambda part: part[k], everything))

    return lax.fori_loop(1, lax.axis_size(axis), step, initial)


def combine_stats(first, second):
    top = jnp.maximum(first[0], second[0])
    total = first[1] * jnp.exp(first[0] - top) + second[1] * jnp.exp(second[0] - top)
    return (top, total)


def shards(queries, keys, values, grad_out, visible, counts):
    row_count, width = queries.shape
    head_dim = width // H
    scale = 1.0 / math.sqrt(head_dim)
    key_all, value_all = (
        lax.all_gather(keys, "tile", axis=0, tiled=True),
        lax.all_gather(values, "tile", axis=0, tiled=True),
    )
    group = key_all.shape[0]
    block_count = counts.shape[0]
    block_keys = group // block_count
    slot_index = jnp.arange(group, dtype=jnp.int32) % block_keys
    key_valid = slot_index < jnp.repeat(counts, block_keys)
    tile_count = visible.shape[0]
    tile_rows = row_count // tile_count
    mask_tiles = (jnp.repeat(visible, block_keys, axis=1) == 1) & key_valid[None, :]
    per_step = 2
    step_count = tile_count // per_step
    step_rows = per_step * tile_rows
    query_blocks = queries.reshape(step_count, step_rows, H, head_dim)
    grad_blocks = grad_out.reshape(step_count, step_rows, H, head_dim)
    mask_blocks = mask_tiles.reshape(step_count, per_step, group)
    key_heads = key_all.reshape(group, H, head_dim)
    value_heads = value_all.reshape(group, H, head_dim)

    def scores_of(query_blk, key_mat):
        return (
            jnp.einsum("qhd,khd->hqk", query_blk, key_mat, preferred_element_type=jnp.float32)
            * scale
        )

    def row_mask(mask_blk):
        return jnp.repeat(mask_blk, tile_rows, axis=0)[None, :, :]

    def local_stats(inputs):
        query_blk, mask_blk = inputs
        scores = scores_of(query_blk, key_heads)
        allowed = row_mask(mask_blk)
        top = jnp.max(jnp.where(allowed, scores, -1e30), axis=-1)
        total = jnp.sum(jnp.where(allowed, jnp.exp(scores - top[..., None]), 0.0), axis=-1)
        return (top, total)

    local_top, local_total = lax.map(local_stats, (query_blocks, mask_blocks))
    global_top, global_total = merged((local_top, local_total), "cam", combine_stats)
    lse_all = global_top + jnp.log(global_total)

    def probs_terms(query_blk, grad_blk, mask_blk, lse_blk, key_mat, value_mat):
        scores = scores_of(query_blk, key_mat)
        allowed = row_mask(mask_blk)
        probs = jnp.where(allowed, jnp.exp(scores - lse_blk[..., None]), 0.0)
        dprobs = jnp.einsum("qhd,khd->hqk", grad_blk, value_mat, preferred_element_type=jnp.float32)
        return (probs, dprobs)

    def local_delta(inputs):
        query_blk, grad_blk, mask_blk, lse_blk = inputs
        probs, dprobs = probs_terms(query_blk, grad_blk, mask_blk, lse_blk, key_heads, value_heads)
        return jnp.sum(probs * dprobs, axis=-1)

    delta_part = lax.map(local_delta, (query_blocks, grad_blocks, mask_blocks, lse_all))
    delta_all = lax.psum(delta_part, "cam")

    def rounded_terms(query_blk, grad_blk, mask_blk, lse_blk, delta_blk, key_mat, value_mat):
        probs, dprobs = probs_terms(query_blk, grad_blk, mask_blk, lse_blk, key_mat, value_mat)
        dscores = probs * (dprobs - delta_blk[..., None])
        return (probs.astype(jnp.bfloat16), dscores.astype(jnp.bfloat16))

    def query_grad_of(dscores_b):
        grad_q = (
            jnp.einsum("hqk,khd->qhd", dscores_b, key_heads, preferred_element_type=jnp.float32)
            * scale
        )
        return grad_q.reshape(step_rows, width)

    def grad_step(carry, inputs):
        query_blk, grad_blk, mask_blk, lse_blk, delta_blk = inputs
        probs_b, dscores_b = rounded_terms(
            query_blk, grad_blk, mask_blk, lse_blk, delta_blk, key_heads, value_heads
        )
        grad_k = (
            carry[0]
            + jnp.einsum("hqk,qhd->khd", dscores_b, query_blk, preferred_element_type=jnp.float32)
            * scale
        )
        grad_v = carry[1] + jnp.einsum(
            "hqk,qhd->khd", probs_b, grad_blk, preferred_element_type=jnp.float32
        )
        return ((grad_k, grad_v), query_grad_of(dscores_b))

    zero_kv = jnp.zeros((group, H, head_dim), jnp.float32)
    (grad_k, grad_v), query_parts = lax.scan(
        grad_step, (zero_kv, zero_kv), (query_blocks, grad_blocks, mask_blocks, lse_all, delta_all)
    )
    joined = jnp.concatenate((grad_k.reshape(group, width), grad_v.reshape(group, width)), axis=1)
    owned = lax.psum_scatter(joined, "tile", scatter_dimension=0, tiled=True)
    grad_queries = lax.psum(query_parts.reshape(row_count, width), "cam").astype(jnp.bfloat16)
    grad_keys = owned[:, :width].astype(jnp.bfloat16)
    grad_values = owned[:, width:].astype(jnp.bfloat16)
    return (grad_queries, grad_keys, grad_values)


def solution(mesh):
    in_specs = (
        P("tile", None),
        P(("cam", "tile"), None),
        P(("cam", "tile"), None),
        P("tile", None),
        P("tile", "cam"),
        P("cam"),
    )
    out_specs = (P("tile", None), P(("cam", "tile"), None), P(("cam", "tile"), None))
    return jax.shard_map(shards, mesh=mesh, in_specs=in_specs, out_specs=out_specs, check_vma=False)
```

profile of v0, /device:TPU:0, one launch (start us, length us, event | category | flops | bytes accessed | tf_op | source)
XLA Modules:
  0.0 218.7 jit_solution(8810301855245995741)
XLA Ops:
  7.2 0.0 reduce-scatter.2.cloned.1.call-start
  7.2 0.7 broadcast_in_dim.79
  7.9 0.1 reshape.121
  8.0 0.7 broadcast_compare_fusion
  8.7 0.1 broadcast_in_dim.78
  8.8 0.1 eq.14
  8.9 45.6 %all_gather.18 = bf16[1024,256]{1,0:T(8,128)(2,1)S(1)} all-gather(bf16[64,256]{1,0:T(8,128)(2,1)} %param.7), channel_id=1, replica_groups=mesh['cam'=2,'tile'=16] {'tile'}, dimensions={0}, use_global_device_ids=true | all-gather | bytes 557056 | tf_op jit(solution)/shard_map/all_gather | solution.py:31
  54.4 0.2 copy.19
  54.7 1.0 copy.18
  55.7 0.1 broadcast_in_dim.80
  55.8 0.0 copy-start.3
  55.8 0.0 copy-start.4
  55.8 1.7 select_reduce_fusion.1
  57.5 0.0 copy-start
  57.5 1.8 all-gather
  59.3 1.4 copy-done
  60.7 2.4 %select_reduce_fusion = f32[8,256]{1,0:T(8,128)S(1)} fusion(f32[8,256,1024]{2,1,0:T(8,128)S(1)} %get-tuple-element.69, f32[8,256]{1,0:T(8,128)S(1)} %get-tuple-element.68, pred[256,1024]{1,0:T(8,128)(4,1)S(1)} %bitcast.24), kind=kLoop, calls=%fused_computation.3 | loop fusion | flops 8386560 | bytes 8667136 | tf_op jit(solution)/shard_map/while/body/eval_jaxpr/reduce_sum | solution.py:65
  63.1 1.8 all-gather.1
  64.9 0.0 copy-done.3
  64.9 0.1 copy.20
  65.0 0.0 copy-done.4
  65.1 38.3 %all_gather.23 = bf16[1024,256]{1,0:T(8,128)(2,1)S(1)} all-gather(bf16[64,256]{1,0:T(8,128)(2,1)S(1)} %copy-done.4), channel_id=1, replica_groups=mesh['cam'=2,'tile'=16] {'tile'}, dimensions={0}, use_global_device_ids=true | all-gather | bytes 557056 | tf_op jit(solution)/shard_map/all_gather | solution.py:32
  103.3 0.2 copy.21
  103.5 0.0 copy-start.1
  103.6 5.7 %fusion.1 = f32[8,1024,32]{1,2,0:T(8,128)} fusion(bf16[256,8,32]{0,2,1:T(8,128)(2,1)S(1)} %bitcast.36, f32[8,256,1024]{2,1,0:T(8,128)} %copy-done, f32[8,256]{1,0:T(8,128)S(1)} %fusion.6, pred[256,1024]{1,0:T(8,128)(4,1)S(1)} %bitcast.25), kind=kOutput, calls=%fused_computation.6 | convolution fusion | flops 142606336 | bytes 9838592 | tf_op jit(solution)/shard_map/while/body/eval_jaxpr/hqk,qhd->khd/dot_general | solution.py:109
  109.3 0.3 copy-done.1
  109.6 5.4 %multiply_reduce_fusion = (f32[8,256]{1,0:T(8,128)S(1)}, f32[8,256,1024]{2,1,0:T(8,128)}) fusion(f32[8,256,1024]{2,1,0:T(8,128)S(1)} %copy-done.1, f32[8,256]{1,0:T(8,128)S(1)} %fusion.6, pred[256,1024]{1,0:T(8,128)(4,1)S(1)} %bitcast.26, bf16[256,8,32]{0,2,1:T(8,128)(2,1)S(1)} %bitcast.37, bf16[1024,8,32]{0,2,1:T(8,128)(2,1)S(1)} %bitcast.31), kind=kOutput, calls=%fused_computation.1 | convolution fusion | flops 144701440 | bytes 17711104 | tf_op jit(solution)/shard_map/while/body/eval_jaxpr/qhd,khd->hqk/dot_general | solution.py:76
  114.9 2.5 %psum.14 = f32[8,256]{1,0:T(8,128)S(1)} all-reduce(f32[8,256]{1,0:T(8,128)S(1)} %get-tuple-element.70), channel_id=1, replica_groups=mesh['cam'=2,'tile'=16] {'cam'}, use_global_device_ids=true, to_apply=%region_3.4 | all-reduce | flops 2048 | bytes 16384 | tf_op jit(solution)/shard_map/psum | solution.py:85
  117.4 7.1 %multiply_convert_fusion = bf16[8,256,1024]{2,1,0:T(8,128)(2,1)S(1)} fusion(f32[8,256,1024]{2,1,0:T(8,128)} %get-tuple-element.71, f32[8,256,1024]{2,1,0:T(8,128)} %copy-done, f32[8,256]{1,0:T(8,128)S(1)} %psum.14, f32[8,256]{1,0:T(8,128)S(1)} %fusion.6, pred[256,1024]{1,0:T(8,128)(4,1)S(1)} %bitcast.27), kind=kLoop, calls=%fused_computation | loop fusion | flops 12582912 | bytes 21250048 | tf_op jit(solution)/shard_map/while/body/eval_jaxpr/convert_element_type | solution.py:90
  124.5 0.0 copy-start.2
  124.5 1.9 copy-done.2
  126.4 0.8 convolution_multiply_fusion
  127.2 0.3 copy.23
  127.6 1.6 copy.24
  129.1 1.7 pad_maximum_fusion
  130.8 0.0 reduce-scatter.2.cloned.1.call-update
  130.8 3.5 %convolution_multiply_fusion.1 = f32[8,256,32]{1,2,0:T(8,128)S(1)} fusion(bf16[8,256,1024]{2,1,0:T(8,128)(2,1)} %copy-done.2, bf16[1024,8,32]{0,2,1:T(8,128)(2,1)S(1)} %bitcast.29), kind=kOutput, calls=%fused_computation.10 | convolution fusion | flops 134283264 | bytes 4980736 | tf_op jit(solution)/shard_map/while/body/eval_jaxpr/hqk,khd->qhd/dot_general | solution.py:94
  134.3 0.1 copy.22
  134.5 4.7 %all-reduce.1 = bf16[256,256]{1,0:T(8,128)(2,1)} all-reduce(f32[256,256]{1,0:T(8,128)S(1)} %copy.22), channel_id=1, replica_groups=mesh['cam'=2,'tile'=16] {'cam'}, use_global_device_ids=true, to_apply=%region_4.5 | all-reduce | flops 65536 | bytes 393216 | tf_op jit(solution)/shard_map/psum | solution.py:120
  139.2 71.1 %reduce-scatter.2.cloned.1.call-done = f32[64,512]{1,0:T(8,128)} async-done(((f32[1024,512]{1,0:T(8,128)}), f32[64,512]{1,0:T(8,128)}) %reduce-scatter.2.cloned.1.call-update) | async-done | bytes 131088 | tf_op jit(solution)/shard_map/reduce_scatter | solution.py:119
  210.3 0.9 convert.4
  211.2 0.6 fusion.14
  (3 shorter events, 0.0 us)
Async XLA Ops:
  7.2 203.2 %reduce-scatter.2.cloned.1.call-start = ((), (), s32[]{:S(2)}) async-start(), calls=%async_computation.1 | async-start | bytes 2228224 | tf_op jit(solution)/shard_map/reduce_scatter | solution.py:119
  55.8 9.2 %copy-start.3 = (bf16[256,256]{1,0:T(8,128)(2,1)S(1)}, bf16[256,256]{1,0:T(8,128)(2,1)}, u32[]{:S(2)}) copy-start(bf16[256,256]{1,0:T(8,128)(2,1)} %param.9) | copy-start | bytes 393220
  55.8 9.3 %copy-start.4 = (bf16[64,256]{1,0:T(8,128)(2,1)S(1)}, bf16[64,256]{1,0:T(8,128)(2,1)}, u32[]{:S(2)}) copy-start(bf16[64,256]{1,0:T(8,128)(2,1)} %param.8) | copy-start | bytes 98308
  57.5 3.2 %copy-start = (f32[8,256,1024]{2,1,0:T(8,128)}, f32[8,256,1024]{2,1,0:T(8,128)S(1)}, u32[]{:S(2)}) copy-start(f32[8,256,1024]{2,1,0:T(8,128)S(1)} %get-tuple-element.69) | copy-start | bytes 25165828
  103.5 6.0 %copy-start.1 = (f32[8,256,1024]{2,1,0:T(8,128)S(1)}, f32[8,256,1024]{2,1,0:T(8,128)}, u32[]{:S(2)}) copy-start(f32[8,256,1024]{2,1,0:T(8,128)} %copy-done) | copy-start | bytes 25165828
  124.5 1.9 copy-start.2
Sparse Core Ops, SparseCore 0:
  130.9 79.3 reduce-scatter.1
where the time goes:
time: 219 us
  blocking collectives  94.6 us (43%)
  waiting for transfers between devices  71.2 us (33%)
  matrix products  17.1 us (8%)
  between operations  14.2 us (6%)
  other arithmetic  12.8 us (6%)
  local copies, waits for them, and re-layouts  8.84 us (4%)
    reduce_scatter x1, waiting for transfers between devices, shards(): owned = lax.psum_scatter(joined, 'tile', scatter_dimension=0, tiled=True)  71.1 us
    all_gather x1, blocking collectives, shards(): lax.all_gather(keys, 'tile', axis=0, tiled=True)  45.6 us
    all_gather x1, blocking collectives, shards(): lax.all_gather(values, 'tile', axis=0, tiled=True)  38.3 us
    convert_element_type x1, other arithmetic, rounded_terms(): return (probs.astype(jnp.bfloat16), dscores.astype(jnp.bfloat16))  7.09 us
    dot_general x1, matrix products, grad_step(): jnp.einsum('hqk,qhd->khd', probs_b, grad_blk, preferred_element_type=jnp....  5.71 us
    dot_general x1, matrix products, probs_terms(): jnp.einsum('qhd,khd->hqk', grad_blk, value_mat, preferred_element_type=jn...  5.35 us
    unnamed x12, local copies, waits for them, and re-layouts  4.72 us
    psum x1, blocking collectives, shards(): lax.psum(query_parts.reshape(row_count, width), 'cam').astype(jnp.bfloat16)  4.69 us
  transfers between devices with their start and end apart: 1, of which 1 were waited for; matrix products, arithmetic and copies ran while one was open for 2% of the time, Pallas kernels for 0%

commit v1 on v0

--- a/solution.py
+++ b/solution.py
@@ -5,6 +5,27 @@
 from jax.sharding import PartitionSpec as P
 
 H = 8
+
+
+def gather_around(x, axis, dim):
+    size, index, rows = (lax.axis_size(axis), lax.axis_index(axis), x.shape[dim])
+    right = [(i, (i + 1) % size) for i in range(size)]
+    downward = [(i, (i - 1) % size) for i in range(size)]
+    whole = jnp.zeros((*x.shape[:dim], size * rows, *x.shape[dim + 1 :]), x.dtype)
+    whole = lax.dynamic_update_slice_in_dim(whole, x, index * rows, axis=dim)
+    from_left = from_right = x
+    halfway = size // 2
+    for turn in range(1, halfway + 1):
+        from_left = lax.ppermute(from_left, axis, right)
+        whole = lax.dynamic_update_slice_in_dim(
+            whole, from_left, (index - turn) % size * rows, axis=dim
+        )
+        if turn < size - halfway:
+            from_right = lax.ppermute(from_right, axis, downward)
+            whole = lax.dynamic_update_slice_in_dim(
+                whole, from_right, (index + turn) % size * rows, axis=dim
+            )
+    return whole
 
 
 def merged(array, axis, combine):
@@ -28,7 +49,7 @@
     head_dim = width // H
     scale = 1.0 / math.sqrt(head_dim)
     key_all, value_all = (
-        lax.all_gather(keys, "tile", axis=0, tiled=True),
+        gather_around(keys, "tile", 0),
         lax.all_gather(values, "tile", axis=0, tiled=True),
     )
     group = key_all.shape[0]

time: 219 us -> 235 us (1.073)
  blocking collectives: 94.6 us -> 55.3 us
  starting transfers between devices: 0.04 us -> 35.7 us
  waiting for transfers between devices: 71.2 us -> 85.3 us
  local copies, waits for them, and re-layouts: 8.84 us -> 18.1 us
  matrix products: 17.1 us -> 13.3 us
    all_gather x1 -> x0, blocking collectives: 45.6 us -> none  [shards(): lax.all_gather(keys, 'tile', axis=0, tiled=True)]
    ppermute x0 -> x15, starting transfers between devices: none -> 35.7 us  [the longest x7 30.6 us: gather_around(): from_right = lax.ppermute(from_right, axis, downward)]
    ppermute x0 -> x15, waiting for transfers between devices: none -> 10.2 us  [the longest x8 7.62 us: gather_around(): from_left = lax.ppermute(from_left, axis, right)]
    dynamic_update_slice x0 -> x16, local copies, waits for them, and re-layouts: none -> 7.19 us  [the longest x8 3.55 us: gather_around(): lax.dynamic_update_slice_in_dim(whole, from_left, (index - turn) % size *...]
    all_gather x1, blocking collectives: 38.3 us -> 44.3 us  [shards(): lax.all_gather(values, 'tile', axis=0, tiled=True)]
    reduce_scatter x1, waiting for transfers between devices: 71.1 us -> 75.1 us  [shards(): owned = lax.psum_scatter(joined, 'tile', scatter_dimension=0, tiled=True)]
    dot_general x1, matrix products: 5.71 us -> 1.78 us  [grad_step(): jnp.einsum('hqk,qhd->khd', probs_b, grad_blk, preferred_element_type=jnp....]
    unnamed x12 -> x7, local copies, waits for them, and re-layouts: 4.72 us -> 4.82 us
  transfers between devices with their start and end apart: 1 -> 16, of which waited for: 1 -> 9; matrix products, arithmetic and copies ran while one was open for 2% -> 7% of each run, Pallas kernels for 0% -> 0%
where the time goes in v1:
time: 235 us
  waiting for transfers between devices  85.3 us (36%)
  blocking collectives  55.3 us (24%)
  starting transfers between devices  35.7 us (15%)
  local copies, waits for them, and re-layouts  18.1 us (8%)
  between operations  14.7 us (6%)
  matrix products  13.3 us (6%)
  other arithmetic  12 us (5%)
    reduce_scatter x1, waiting for transfers between devices, shards(): owned = lax.psum_scatter(joined, 'tile', scatter_dimension=0, tiled=True)  75.1 us
    all_gather x1, blocking collectives, shards(): lax.all_gather(values, 'tile', axis=0, tiled=True)  44.3 us
    ppermute x7, starting transfers between devices, gather_around(): from_right = lax.ppermute(from_right, axis, downward)  30.6 us
    ppermute x8, waiting for transfers between devices, gather_around(): from_left = lax.ppermute(from_left, axis, right)  7.62 us
    convert_element_type x1, other arithmetic, rounded_terms(): return (probs.astype(jnp.bfloat16), dscores.astype(jnp.bfloat16))  7.03 us
    ppermute x8, starting transfers between devices, gather_around(): from_left = lax.ppermute(from_left, axis, right)  5.06 us
    unnamed x7, local copies, waits for them, and re-layouts  4.82 us
    dot_general x1, matrix products, probs_terms(): jnp.einsum('qhd,khd->hqk', grad_blk, value_mat, preferred_element_type=jn...  4.74 us
  transfers between devices with their start and end apart: 16, of which 9 were waited for; matrix products, arithmetic and copies ran while one was open for 7% of the time, Pallas kernels for 0%

profile of v1, /device:TPU:0, one launch (start us, length us, event | category | flops | bytes accessed | tf_op | source)
XLA Modules:
  0.0 234.5 jit_solution(3633510461998323467)
XLA Ops:
  7.2 3.0 %collective-permute-start = (bf16[64,256]{1,0:T(8,128)(2,1)}, bf16[64,256]{1,0:T(8,128)(2,1)S(1)}, u32[]{:S(2)}, u32[]{:S(2)}) collective-permute-start(bf16[64,256]{1,0:T(8,128)(2,1)} %param.7), channel_id=1, source_target_pairs={{0,1},{1,2},{2,3},{3,4},{4,5},{5,6},{6,7},{7,8},{8,9},{9,10},{10,1... | collective-permute-start | bytes 98312 | tf_op jit(solution)/shard_map/ppermute | solution.py:19
  10.2 4.1 %collective-permute-start.1 = (bf16[64,256]{1,0:T(8,128)(2,1)}, bf16[64,256]{1,0:T(8,128)(2,1)S(1)}, u32[]{:S(2)}, u32[]{:S(2)}) collective-permute-start(bf16[64,256]{1,0:T(8,128)(2,1)} %param.7), channel_id=1, source_target_pairs={{0,15},{1,0},{2,1},{3,2},{4,3},{5,4},{6,5},{7,6},{8,7},{9,8},{10,9... | collective-permute-start | bytes 98312 | tf_op jit(solution)/shard_map/ppermute | solution.py:24
  14.3 2.0 collective-permute-done
  16.3 5.7 %collective-permute-start.3 = (bf16[64,256]{1,0:T(8,128)(2,1)S(1)}, bf16[64,256]{1,0:T(8,128)(2,1)S(1)}, u32[]{:S(2)}, u32[]{:S(2)}) collective-permute-start(bf16[64,256]{1,0:T(8,128)(2,1)S(1)} %collective-permute-done.1), channel_id=1, source_target_pairs={{0,15},{1,0},{2,1},{3,2},{4,3},{5,4},{6,5},{7,6},{8,7},{9,8},{10,9... | collective-permute-start | bytes 98312 | tf_op jit(solution)/shard_map/ppermute | solution.py:24
  22.0 1.8 collective-permute-done.2
  23.8 5.7 %collective-permute-start.5 = (bf16[64,256]{1,0:T(8,128)(2,1)S(1)}, bf16[64,256]{1,0:T(8,128)(2,1)S(1)}, u32[]{:S(2)}, u32[]{:S(2)}) collective-permute-start(bf16[64,256]{1,0:T(8,128)(2,1)S(1)} %collective-permute-done.3), channel_id=1, source_target_pairs={{0,15},{1,0},{2,1},{3,2},{4,3},{5,4},{6,5},{7,6},{8,7},{9,8},{10,9... | collective-permute-start | bytes 98312 | tf_op jit(solution)/shard_map/ppermute | solution.py:24
  29.5 1.8 collective-permute-done.4
  31.4 5.7 %collective-permute-start.7 = (bf16[64,256]{1,0:T(8,128)(2,1)S(1)}, bf16[64,256]{1,0:T(8,128)(2,1)S(1)}, u32[]{:S(2)}, u32[]{:S(2)}) collective-permute-start(bf16[64,256]{1,0:T(8,128)(2,1)S(1)} %collective-permute-done.5), channel_id=1, source_target_pairs={{0,15},{1,0},{2,1},{3,2},{4,3},{5,4},{6,5},{7,6},{8,7},{9,8},{10,9... | collective-permute-start | bytes 98312 | tf_op jit(solution)/shard_map/ppermute | solution.py:24
  37.1 1.8 collective-permute-done.6
  38.9 44.3 %all_gather.19 = bf16[1024,256]{1,0:T(8,128)(2,1)S(1)} all-gather(bf16[64,256]{1,0:T(8,128)(2,1)} %param.8), channel_id=1, replica_groups=mesh['cam'=2,'tile'=16] {'tile'}, dimensions={0}, use_global_device_ids=true | all-gather | bytes 557056 | tf_op jit(solution)/shard_map/all_gather | solution.py:53
  83.2 0.7 broadcast_in_dim.83
  84.0 2.0 collective-permute-start.10
  86.1 1.9 collective-permute-done.9
  87.9 3.6 %collective-permute-start.11 = (bf16[64,256]{1,0:T(8,128)(2,1)S(1)}, bf16[64,256]{1,0:T(8,128)(2,1)S(1)}, u32[]{:S(2)}, u32[]{:S(2)}) collective-permute-start(bf16[64,256]{1,0:T(8,128)(2,1)S(1)} %collective-permute-done.9), channel_id=1, source_target_pairs={{0,15},{1,0},{2,1},{3,2},{4,3},{5,4},{6,5},{7,6},{8,7},{9,8},{10,9... | collective-permute-start | bytes 98312 | tf_op jit(solution)/shard_map/ppermute | solution.py:24
  91.6 0.7 broadcast_compare_fusion
  92.5 0.7 collective-permute-done.11
  93.1 5.9 %collective-permute-start.13 = (bf16[64,256]{1,0:T(8,128)(2,1)S(1)}, bf16[64,256]{1,0:T(8,128)(2,1)S(1)}, u32[]{:S(2)}, u32[]{:S(2)}) collective-permute-start(bf16[64,256]{1,0:T(8,128)(2,1)S(1)} %collective-permute-done.11), channel_id=1, source_target_pairs={{0,15},{1,0},{2,1},{3,2},{4,3},{5,4},{6,5},{7,6},{8,7},{9,8},{10,9... | collective-permute-start | bytes 98312 | tf_op jit(solution)/shard_map/ppermute | solution.py:24
  99.1 0.9 copy.39
  100.3 0.4 copy.55
  100.8 1.0 copy.56
  101.8 1.0 copy.57
  103.2 0.3 dynamic_update_slice.58
  103.6 0.5 dynamic_update_slice.59
  104.3 0.6 dynamic_update_slice.60
  105.9 0.6 dynamic_update_slice.63
  106.6 0.6 dynamic_update_slice.64
  108.2 0.6 dynamic_update_slice.67
  108.9 0.6 dynamic_update_slice.68
  110.5 0.6 dynamic_update_slice.71
  111.2 0.6 dynamic_update_slice.72
  112.3 1.5 fusion
  113.8 2.0 all-gather
  115.8 1.7 fusion.3
  117.5 1.8 all-gather.1
  119.4 1.8 fusion.7
  121.1 4.7 %multiply_reduce_fusion = (f32[8,256]{1,0:T(8,128)S(1)}, f32[8,256,1024]{1,2,0:T(8,128)}) fusion(f32[8,1024,256]{2,1,0:T(8,128)S(1)} %get-tuple-element.69, f32[8,256]{1,0:T(8,128)S(1)} %fusion.12, pred[256,1024]{0,1:T(8,128)(4,1)S(1)} %copy.55, bf16[256,8,32]{0,2,1:T(8,128)(2,1)S(1)} %bitcast.56, bf16[1024,8,32]{0,2,1:T(8,128)(2,1)S(1)} %bitcast.49), kind=kOutput, calls=%fused_computation.10 | convolution fusion | flops 144701440 | bytes 17711104 | tf_op jit(solution)/shard_map/while/body/eval_jaxpr/qhd,khd->hqk/dot_general | solution.py:97
  125.9 2.5 %psum.14 = f32[8,256]{1,0:T(8,128)S(1)} all-reduce(f32[8,256]{1,0:T(8,128)S(1)} %get-tuple-element.70), channel_id=1, replica_groups=mesh['cam'=2,'tile'=16] {'cam'}, use_global_device_ids=true, to_apply=%region_3.4 | all-reduce | flops 2048 | bytes 16384 | tf_op jit(solution)/shard_map/psum | solution.py:106
  128.3 0.3 copy.66
  128.7 7.0 %multiply_convert_fusion = bf16[8,256,1024]{1,2,0:T(8,128)(2,1)S(1)} fusion(f32[8,256,1024]{1,2,0:T(8,128)} %get-tuple-element.71, f32[8,1024,256]{2,1,0:T(8,128)} %copy-done, f32[8,256]{1,0:T(8,128)S(1)} %psum.14, f32[8,256]{1,0:T(8,128)S(1)} %fusion.12, pred[256,1024]{0,1:T(8,128)(4,1)S(1)} %copy.55), kind=kLoop, calls=%fused_computation.9 | loop fusion | flops 12582912 | bytes 21250048 | tf_op jit(solution)/shard_map/while/body/eval_jaxpr/convert_element_type | solution.py:111
  135.7 1.9 copy-done.1
  137.7 2.3 convolution_multiply_fusion
  140.0 1.6 copy.65
  141.5 1.6 pad_maximum_fusion
  143.2 3.0 %convolution_multiply_fusion.1 = f32[8,32,256]{2,1,0:T(8,128)S(1)} fusion(bf16[1024,8,32]{0,2,1:T(8,128)(2,1)S(1)} %bitcast.47, bf16[8,256,1024]{1,2,0:T(8,128)(2,1)} %copy-done.1), kind=kOutput, calls=%fused_computation.16 | convolution fusion | flops 134283264 | bytes 4980736 | tf_op jit(solution)/shard_map/while/body/eval_jaxpr/hqk,khd->qhd/dot_general | solution.py:115
  146.3 4.7 %all-reduce.1 = bf16[256,256]{1,0:T(8,128)(2,1)} all-reduce(f32[256,256]{1,0:T(8,128)S(1)} %copy.62), channel_id=1, replica_groups=mesh['cam'=2,'tile'=16] {'cam'}, use_global_device_ids=true, to_apply=%region_4.5 | all-reduce | flops 65536 | bytes 393216 | tf_op jit(solution)/shard_map/psum | solution.py:141
  151.0 75.1 %reduce-scatter.2.cloned.1.call-done = f32[64,512]{1,0:T(8,128)} async-done(((f32[1024,512]{1,0:T(8,128)}), f32[64,512]{1,0:T(8,128)}) %reduce-scatter.2.cloned.1.call-update) | async-done | bytes 131088 | tf_op jit(solution)/shard_map/reduce_scatter | solution.py:140
  226.1 0.9 convert.4
  227.1 0.6 fusion.20
  (53 shorter events, 4.8 us)
Async XLA Ops:
  7.2 219.0 %reduce-scatter.2.cloned.1.call-start = ((), (), s32[]{:S(2)}) async-start(), calls=%async_computation.1 | async-start | bytes 2228224 | tf_op jit(solution)/shard_map/reduce_scatter | solution.py:140
  7.2 9.1 %collective-permute-start = (bf16[64,256]{1,0:T(8,128)(2,1)}, bf16[64,256]{1,0:T(8,128)(2,1)S(1)}, u32[]{:S(2)}, u32[]{:S(2)}) collective-permute-start(bf16[64,256]{1,0:T(8,128)(2,1)} %param.7), channel_id=1, source_target_pairs={{0,1},{1,2},{2,3},{3,4},{4,5},{5,6},{6,7},{7,8},{8,9},{9,10},{10,1... | collective-permute-start | bytes 98312 | tf_op jit(solution)/shard_map/ppermute | solution.py:19
  10.2 6.1 %collective-permute-start.1 = (bf16[64,256]{1,0:T(8,128)(2,1)}, bf16[64,256]{1,0:T(8,128)(2,1)S(1)}, u32[]{:S(2)}, u32[]{:S(2)}) collective-permute-start(bf16[64,256]{1,0:T(8,128)(2,1)} %param.7), channel_id=1, source_target_pairs={{0,15},{1,0},{2,1},{3,2},{4,3},{5,4},{6,5},{7,6},{8,7},{9,8},{10,9... | collective-permute-start | bytes 98312 | tf_op jit(solution)/shard_map/ppermute | solution.py:24
  16.3 7.5 %collective-permute-start.2 = (bf16[64,256]{1,0:T(8,128)(2,1)S(1)}, bf16[64,256]{1,0:T(8,128)(2,1)S(1)}, u32[]{:S(2)}, u32[]{:S(2)}) collective-permute-start(bf16[64,256]{1,0:T(8,128)(2,1)S(1)} %collective-permute-done), channel_id=1, source_target_pairs={{0,1},{1,2},{2,3},{3,4},{4,5},{5,6},{6,7},{7,8},{8,9},{9,10},{10,1... | collective-permute-start | bytes 98312 | tf_op jit(solution)/shard_map/ppermute | solution.py:19
  16.3 7.5 %collective-permute-start.3 = (bf16[64,256]{1,0:T(8,128)(2,1)S(1)}, bf16[64,256]{1,0:T(8,128)(2,1)S(1)}, u32[]{:S(2)}, u32[]{:S(2)}) collective-permute-start(bf16[64,256]{1,0:T(8,128)(2,1)S(1)} %collective-permute-done.1), channel_id=1, source_target_pairs={{0,15},{1,0},{2,1},{3,2},{4,3},{5,4},{6,5},{7,6},{8,7},{9,8},{10,9... | collective-permute-start | bytes 98312 | tf_op jit(solution)/shard_map/ppermute | solution.py:24
  23.8 7.5 %collective-permute-start.4 = (bf16[64,256]{1,0:T(8,128)(2,1)S(1)}, bf16[64,256]{1,0:T(8,128)(2,1)S(1)}, u32[]{:S(2)}, u32[]{:S(2)}) collective-permute-start(bf16[64,256]{1,0:T(8,128)(2,1)S(1)} %collective-permute-done.2), channel_id=1, source_target_pairs={{0,1},{1,2},{2,3},{3,4},{4,5},{5,6},{6,7},{7,8},{8,9},{9,10},{10,1... | collective-permute-start | bytes 98312 | tf_op jit(solution)/shard_map/ppermute | solution.py:19
  23.8 7.5 %collective-permute-start.5 = (bf16[64,256]{1,0:T(8,128)(2,1)S(1)}, bf16[64,256]{1,0:T(8,128)(2,1)S(1)}, u32[]{:S(2)}, u32[]{:S(2)}) collective-permute-start(bf16[64,256]{1,0:T(8,128)(2,1)S(1)} %collective-permute-done.3), channel_id=1, source_target_pairs={{0,15},{1,0},{2,1},{3,2},{4,3},{5,4},{6,5},{7,6},{8,7},{9,8},{10,9... | collective-permute-start | bytes 98312 | tf_op jit(solution)/shard_map/ppermute | solution.py:24
  31.4 7.5 %collective-permute-start.6 = (bf16[64,256]{1,0:T(8,128)(2,1)S(1)}, bf16[64,256]{1,0:T(8,128)(2,1)S(1)}, u32[]{:S(2)}, u32[]{:S(2)}) collective-permute-start(bf16[64,256]{1,0:T(8,128)(2,1)S(1)} %collective-permute-done.4), channel_id=1, source_target_pairs={{0,1},{1,2},{2,3},{3,4},{4,5},{5,6},{6,7},{7,8},{8,9},{9,10},{10,1... | collective-permute-start | bytes 98312 | tf_op jit(solution)/shard_map/ppermute | solution.py:19
  31.4 52.7 %collective-permute-start.7 = (bf16[64,256]{1,0:T(8,128)(2,1)S(1)}, bf16[64,256]{1,0:T(8,128)(2,1)S(1)}, u32[]{:S(2)}, u32[]{:S(2)}) collective-permute-start(bf16[64,256]{1,0:T(8,128)(2,1)S(1)} %collective-permute-done.5), channel_id=1, source_target_pairs={{0,15},{1,0},{2,1},{3,2},{4,3},{5,4},{6,5},{7,6},{8,7},{9,8},{10,9... | collective-permute-start | bytes 98312 | tf_op jit(solution)/shard_map/ppermute | solution.py:24
  38.9 45.1 %collective-permute-start.8 = (bf16[64,256]{1,0:T(8,128)(2,1)S(1)}, bf16[64,256]{1,0:T(8,128)(2,1)S(1)}, u32[]{:S(2)}, u32[]{:S(2)}) collective-permute-start(bf16[64,256]{1,0:T(8,128)(2,1)S(1)} %collective-permute-done.6), channel_id=1, source_target_pairs={{0,1},{1,2},{2,3},{3,4},{4,5},{5,6},{6,7},{7,8},{8,9},{9,10},{10,1... | collective-permute-start | bytes 98312 | tf_op jit(solution)/shard_map/ppermute | solution.py:19
  84.0 3.9 %collective-permute-start.9 = (bf16[64,256]{1,0:T(8,128)(2,1)S(1)}, bf16[64,256]{1,0:T(8,128)(2,1)S(1)}, u32[]{:S(2)}, u32[]{:S(2)}) collective-permute-start(bf16[64,256]{1,0:T(8,128)(2,1)S(1)} %collective-permute-done.7), channel_id=1, source_target_pairs={{0,15},{1,0},{2,1},{3,2},{4,3},{5,4},{6,5},{7,6},{8,7},{9,8},{10,9... | collective-permute-start | bytes 98312 | tf_op jit(solution)/shard_map/ppermute | solution.py:24
  84.0 7.6 %collective-permute-start.10 = (bf16[64,256]{1,0:T(8,128)(2,1)S(1)}, bf16[64,256]{1,0:T(8,128)(2,1)S(1)}, u32[]{:S(2)}, u32[]{:S(2)}) collective-permute-start(bf16[64,256]{1,0:T(8,128)(2,1)S(1)} %collective-permute-done.8), channel_id=1, source_target_pairs={{0,1},{1,2},{2,3},{3,4},{4,5},{5,6},{6,7},{7,8},{8,9},{9,10},{10,1... | collective-permute-start | bytes 98312 | tf_op jit(solution)/shard_map/ppermute | solution.py:19
  87.9 5.2 %collective-permute-start.11 = (bf16[64,256]{1,0:T(8,128)(2,1)S(1)}, bf16[64,256]{1,0:T(8,128)(2,1)S(1)}, u32[]{:S(2)}, u32[]{:S(2)}) collective-permute-start(bf16[64,256]{1,0:T(8,128)(2,1)S(1)} %collective-permute-done.9), channel_id=1, source_target_pairs={{0,15},{1,0},{2,1},{3,2},{4,3},{5,4},{6,5},{7,6},{8,7},{9,8},{10,9... | collective-permute-start | bytes 98312 | tf_op jit(solution)/shard_map/ppermute | solution.py:24
  91.6 7.5 %collective-permute-start.12 = (bf16[64,256]{1,0:T(8,128)(2,1)S(1)}, bf16[64,256]{1,0:T(8,128)(2,1)S(1)}, u32[]{:S(2)}, u32[]{:S(2)}) collective-permute-start(bf16[64,256]{1,0:T(8,128)(2,1)S(1)} %collective-permute-done.10), channel_id=1, source_target_pairs={{0,1},{1,2},{2,3},{3,4},{4,5},{5,6},{6,7},{7,8},{8,9},{9,10},{10,1... | collective-permute-start | bytes 98312 | tf_op jit(solution)/shard_map/ppermute | solution.py:19
  93.1 18.0 %collective-permute-start.13 = (bf16[64,256]{1,0:T(8,128)(2,1)S(1)}, bf16[64,256]{1,0:T(8,128)(2,1)S(1)}, u32[]{:S(2)}, u32[]{:S(2)}) collective-permute-start(bf16[64,256]{1,0:T(8,128)(2,1)S(1)} %collective-permute-done.11), channel_id=1, source_target_pairs={{0,15},{1,0},{2,1},{3,2},{4,3},{5,4},{6,5},{7,6},{8,7},{9,8},{10,9... | collective-permute-start | bytes 98312 | tf_op jit(solution)/shard_map/ppermute | solution.py:24
  99.1 12.7 %collective-permute-start.14 = (bf16[64,256]{1,0:T(8,128)(2,1)S(1)}, bf16[64,256]{1,0:T(8,128)(2,1)S(1)}, u32[]{:S(2)}, u32[]{:S(2)}) collective-permute-start(bf16[64,256]{1,0:T(8,128)(2,1)S(1)} %collective-permute-done.12), channel_id=1, source_target_pairs={{0,1},{1,2},{2,3},{3,4},{4,5},{5,6},{6,7},{7,8},{8,9},{9,10},{10,1... | collective-permute-start | bytes 98312 | tf_op jit(solution)/shard_map/ppermute | solution.py:19
  113.8 7.4 %copy-start = (f32[8,1024,256]{2,1,0:T(8,128)}, f32[8,1024,256]{2,1,0:T(8,128)S(1)}, u32[]{:S(2)}) copy-start(f32[8,1024,256]{2,1,0:T(8,128)S(1)} %get-tuple-element.69) | copy-start | bytes 25165828
  135.7 1.9 copy-start.1
Sparse Core Ops, SparseCore 0:
  143.3 82.7 reduce-scatter.1
